TPU v7x, 512 devices: a whole 4x4x16 slice. The times are simulated.
512 devices in a mesh: ctx: 16 (over y, z_hi), exp: 16 (over x, z_lo), dp: 2 (over core).
Axes of the slice: x: 4, y: 4, z: 16 (z_hi: 4, z_lo: 4; z = z_hi * 4 + z_lo), core: 2. Of those that a mesh axis runs over, the one named last changes fastest.
Arguments:
- queries: bfloat16 [32, 3072, 2048], P(('dp', 'exp'), 'ctx'), parts along dimension 0, may hold values from -38 to 38
- keys: bfloat16 [32, 3072, 256], P(('dp', 'exp'), 'ctx'), parts along dimension 0, may hold values from -4 to 4
- values: bfloat16 [32, 3072, 256], P(('dp', 'exp'), 'ctx'), parts along dimension 0, may hold values from -6 to 6
- segments: int32 [32, 3072], P(('dp', 'exp')), parts along dimension 0, may hold values from 0 to 7, never falling along the last dimension, each value on 1 to 1536 neighbouring positions
- residual: bfloat16 [32, 3072, 1024], P(('dp', 'exp'), 'ctx'), parts along dimension 0, may hold values from -3 to 3
- out_weight: bfloat16 [2048, 1024], P('ctx'), may hold values from -0.125 to 0.125
- gain: float32 [1024], replicated, may hold values from 0.1 to 1.9
- expert_ids: int32 [32, 3072, 8], P(('dp', 'exp'), 'ctx'), parts along dimension 0, may hold values from 0 to 127, all different within a row; in each aligned block of 192 rows (0 to 191, 192 to 383, ..., all dimensions but the last counted through in order) at most 24 rows name the same one
- route_weights: float32 [32, 3072, 8], P(('dp', 'exp'), 'ctx'), parts along dimension 0, may hold values from 0.05 to 0.5
- w_gate: bfloat16 [16, 1024, 384], P('exp'), may hold values from -0.1875 to 0.1875
- w_up: bfloat16 [16, 1024, 384], P('exp'), may hold values from -0.1875 to 0.1875
- w_down: bfloat16 [16, 384, 1024], P('exp'), may hold values from -0.3125 to 0.3125
Outputs:
- layer_out: bfloat16 [32, 3072, 1024], P(('dp', 'exp'), 'ctx'), parts along dimension 0
There are 2 independent parts, one for each index of `dp`. A program takes and returns all parts, laid end to end along the dimension named above; an argument that names none is the same for every part. Nothing has to cross between parts.
Inputs may be any that keep to these rules, and one draw needn't show every extreme that they name: `expert_ids`: in every aligned block of 192 positions of a sequence (one slab), no expert is named by more than 24 tokens, and in every draw some expert is named by exactly 24 tokens of some block; a token names 8 different experts. `segments`: document numbers never fall along a sequence.
All inputs are finite; a program needn't handle non-finite values.
Results may differ from a plain program's by a relative error of at most 0.006.
Values may be sent and summed in bfloat16 or wider, within the bound.
A program may use at most 64 MiB of HBM per device.

v0:
```python
import math
import jax
import jax.numpy as jnp
from jax import lax
from jax.sharding import PartitionSpec as P

HQ = 16
KVH = 2
HD = 128
TOP = 8
CAP = 24


def per_device(
    queries,
    keys,
    values,
    segments,
    residual,
    out_weight,
    gain,
    expert_ids,
    route_weights,
    w_gate,
    w_up,
    w_down,
):
    tok_rows = queries.shape[1]
    model_width = residual.shape[2]
    groups = HQ // KVH
    scale_factor = 1.0 / math.sqrt(HD)
    rank_ctx = lax.axis_index("ctx")
    query_pos = rank_ctx * tok_rows + jnp.arange(tok_rows, dtype=jnp.int32)
    seg_line = segments[0]
    query_seg = lax.dynamic_slice_in_dim(seg_line, rank_ctx * tok_rows, tok_rows)
    query_heads = queries[0].reshape(tok_rows, KVH, groups, HD)

    def attend_block(running, inputs):
        key_blk, value_blk, blk_start = inputs
        blk_rows = key_blk.shape[0]
        key_pos = blk_start + jnp.arange(blk_rows, dtype=jnp.int32)
        key_seg = lax.dynamic_slice_in_dim(seg_line, blk_start, blk_rows)
        run_max, run_sum, accum = running
        scores = (
            jnp.einsum("qkgd,skd->qkgs", query_heads, key_blk, preferred_element_type=jnp.float32)
            * scale_factor
        )
        allowed = (
            (key_pos[None, :] <= query_pos[:, None]) & (key_seg[None, :] == query_seg[:, None])
        )[:, None, None, :]
        masked_scores = jnp.where(allowed, scores, -1e30)
        new_max = jnp.maximum(run_max, jnp.max(masked_scores, axis=-1))
        correction = jnp.exp(run_max - new_max)
        expo = jnp.where(allowed, jnp.exp(scores - new_max[..., None]), 0.0)
        new_sum = run_sum * correction + jnp.sum(expo, axis=-1)
        probs = expo.astype(jnp.bfloat16)
        new_accum = accum * correction[..., None] + jnp.einsum(
            "qkgs,skd->qkgd", probs, value_blk, preferred_element_type=jnp.float32
        )
        updated = (new_max, new_sum, new_accum)
        return (updated, None)

    initial = (
        jnp.full((tok_rows, KVH, groups), -1e30, jnp.float32),
        jnp.zeros((tok_rows, KVH, groups), jnp.float32),
        jnp.zeros((tok_rows, KVH, groups, HD), jnp.float32),
    )
    running = initial
    key_piece = lax.all_gather(keys, "ctx", axis=1, tiled=True)
    value_piece = lax.all_gather(values, "ctx", axis=1, tiled=True)
    row_count = key_piece.shape[1]
    blk_rows = math.gcd(row_count, 512)
    blk_count = row_count // blk_rows
    key_blocks = key_piece[0].reshape(blk_count, blk_rows, KVH, HD)
    value_blocks = value_piece[0].reshape(blk_count, blk_rows, KVH, HD)
    blk_starts = blk_rows * jnp.arange(blk_count, dtype=jnp.int32)
    running, _ = lax.scan(attend_block, running, (key_blocks, value_blocks, blk_starts))
    run_max, run_sum, accum = running
    attended = (accum / run_sum[..., None]).reshape(tok_rows, HQ * HD).astype(jnp.bfloat16)
    projected = jnp.dot(
        attended,
        lax.all_gather(out_weight, "ctx", axis=0, tiled=True),
        preferred_element_type=jnp.float32,
    )
    hidden_state = residual[0].astype(jnp.float32) + projected
    normed = (
        hidden_state
        * lax.rsqrt(jnp.mean(hidden_state * hidden_state, axis=-1, keepdims=True) + 1e-06)
        * gain
    ).astype(jnp.bfloat16)
    owners = lax.axis_size("exp")
    chosen = expert_ids[0]
    active = chosen < owners
    owner_range = jnp.arange(owners, dtype=jnp.int32)
    hit_table = (
        ((chosen[:, :, None] == owner_range) & active[:, :, None])
        .astype(jnp.int32)
        .reshape(tok_rows * TOP, owners)
    )
    rank_in = jnp.sum((jnp.cumsum(hit_table, axis=0) - 1) * hit_table, axis=1).reshape(
        tok_rows, TOP
    )
    slot_total = owners * CAP
    slot_of = jnp.where(active, chosen * CAP + rank_in, slot_total)
    slot_range = jnp.arange(slot_total, dtype=jnp.int32)
    placing = jnp.any(slot_of[None, :, :] == slot_range[:, None, None], axis=2).astype(jnp.bfloat16)
    outgoing = (
        jnp.dot(placing, normed, preferred_element_type=jnp.float32)
        .astype(jnp.bfloat16)
        .reshape(owners, CAP, model_width)
    )
    arrived = lax.all_to_all(outgoing, "exp", split_axis=0, concat_axis=0, tiled=True)
    item_count = arrived.shape[1]
    flat_rows = arrived.reshape(owners * item_count, model_width)
    gate_part = jnp.dot(flat_rows, w_gate[0], preferred_element_type=jnp.float32)
    up_part = jnp.dot(flat_rows, w_up[0], preferred_element_type=jnp.float32)
    expert_hidden = (jax.nn.silu(gate_part) * up_part).astype(jnp.bfloat16)
    expert_out = jnp.dot(expert_hidden, w_down[0], preferred_element_type=jnp.float32).astype(
        jnp.bfloat16
    )
    returned = lax.all_to_all(
        expert_out.reshape(owners, item_count, model_width),
        "exp",
        split_axis=0,
        concat_axis=0,
        tiled=True,
    )
    padded_back = jnp.concatenate(
        [returned.reshape(slot_total, model_width), jnp.zeros((1, model_width), jnp.bfloat16)],
        axis=0,
    )
    picked = padded_back[slot_of]
    mix_weights = jnp.where(active, route_weights[0], 0.0)
    moe_sum = jnp.einsum("tk,tkd->td", mix_weights, picked.astype(jnp.float32))
    layer_out = (hidden_state + moe_sum).astype(jnp.bfloat16)
    return layer_out[None]


def solution(mesh):
    return jax.shard_map(
        per_device,
        mesh=mesh,
        in_specs=(
            P(("dp", "exp"), "ctx", None),
            P(("dp", "exp"), "ctx", None),
            P(("dp", "exp"), "ctx", None),
            P(("dp", "exp"), None),
            P(("dp", "exp"), "ctx", None),
            P("ctx", None),
            P(),
            P(("dp", "exp"), "ctx", None),
            P(("dp", "exp"), "ctx", None),
            P("exp", None, None),
            P("exp", None, None),
            P("exp", None, None),
        ),
        out_specs=P(("dp", "exp"), "ctx", None),
        check_vma=False,
    )
```

profile of v0, /device:TPU:1, one launch (start us, length us, event | category | flops | bytes accessed | tf_op | source)
XLA Modules:
  0.0 393.0 jit_solution(8537777085268056994)
XLA Ops:
  10.4 4.5 %reduce-window.6 = s32[16,12,128]{2,1,0:T(8,128)S(1)} reduce-window(s32[16,12,128]{2,1,0:T(8,128)S(1)} %fusion.41, s32[]{:T(128)} %constant.11.clone.1), window={size=1x1x128 pad=0_0x0_0x127_0}, to_apply=%region_4.5 | reduce-window | flops 3121152 | bytes 196612 | tf_op jit(solution)/shard_map/reduce-window
  20.8 79.8 %all-gather.6.cloned.1.call-done = bf16[1,3072,256]{2,1,0:T(8,128)(2,1)} async-done(((bf16[1,192,256]{2,1,0:T(8,128)(2,1)}), bf16[1,3072,256]{2,1,0:T(8,128)(2,1)}) %all-gather.6.cloned.1.call-update) | async-done | bytes 1572880 | tf_op jit(solution)/shard_map/all_gather | solution.py:70
  103.0 81.9 %all-gather.4.cloned.1.call-done = bf16[1,3072,256]{2,1,0:T(8,128)(2,1)} async-done(((bf16[1,192,256]{2,1,0:T(8,128)(2,1)}), bf16[1,3072,256]{2,1,0:T(8,128)(2,1)}) %all-gather.4.cloned.1.call-update) | async-done | bytes 1572880 | tf_op jit(solution)/shard_map/all_gather | solution.py:69
  188.3 116.4 %while.15 = (s32[]{:T(128)}, f32[192,2,8]{0,2,1:T(8,128)S(1)}, f32[192,2,8]{0,2,1:T(8,128)S(1)}, f32[192,2,8,128]{3,0,2,1:T(8,128)}, s32[6]{0:T(128)}, /*index=5...) while((s32[]{:T(128)}, f32[192,2,8]{0,2,1:T(8,128)S(1)}, ...), condition=%wide.region_3.4_spmd.clone, body=%wide.region_0.3_spmd.clone.sunk | while | flops 824098496 | bytes 50147816 | solution.py:77
  198.7 4.3 %fusion.61 = f32[192,2,8]{0,2,1:T(8,128)S(1)} fusion(f32[2,512,192,8]{1,2,3,0:T(8,128)} %get-tuple-element.231, f32[192,2,8]{0,2,1:T(8,128)S(1)} %select_maximum_fusion.2, pred[192,512]{1,0:T(8,128)(4,1)S(1)} %compare_and_fusion.2), kind=kLoop, calls=%fused_computation.8.clone.1 | loop fusion | flops 6288384 | bytes 6414336 | tf_op jit(solution)/shard_map/while/body/eval_jaxpr/reduce_sum | solution.py:55
  213.3 3.7 fusion.60
  217.1 4.3 %fusion.61 = f32[192,2,8]{0,2,1:T(8,128)S(1)} fusion(f32[2,512,192,8]{1,2,3,0:T(8,128)} %get-tuple-element.231, f32[192,2,8]{0,2,1:T(8,128)S(1)} %select_maximum_fusion.2, pred[192,512]{1,0:T(8,128)(4,1)S(1)} %compare_and_fusion.2), kind=kLoop, calls=%fused_computation.8.clone.1 | loop fusion | flops 6288384 | bytes 6414336 | tf_op jit(solution)/shard_map/while/body/eval_jaxpr/reduce_sum | solution.py:55
  221.7 4.5 %bitcast_add_fusion.4 = f32[192,2,8,128]{3,0,2,1:T(8,128)} fusion(f32[192,2,8,128]{3,0,2,1:T(8,128)} %get-tuple-element.252, f32[2,512,192,8]{1,2,3,0:T(8,128)S(1)} %copy-done.1, f32[192,2,8]{0,2,1:T(8,128)S(1)} %select_maximum_fusion.2, pred[192,512]{1,0:T(8,128)(4,1)S(1)} %compare_and_fusion.2, f32[192,2,8]{0,2,1:T(8,128)S(1)} %get-tuple-element.233, ...), kind=kOutput, calls=%fused_computation.14.clone.1 | convolution fusion | flops 410124288 | bytes 9822209 | tf_op jit(solution)/shard_map/while/body/eval_jaxpr/qkgs,skd->qkgd/dot_general | solution.py:57
  232.9 3.7 fusion.60
  236.7 4.3 %fusion.61 = f32[192,2,8]{0,2,1:T(8,128)S(1)} fusion(f32[2,512,192,8]{1,2,3,0:T(8,128)} %get-tuple-element.231, f32[192,2,8]{0,2,1:T(8,128)S(1)} %select_maximum_fusion.2, pred[192,512]{1,0:T(8,128)(4,1)S(1)} %compare_and_fusion.2), kind=kLoop, calls=%fused_computation.8.clone.1 | loop fusion | flops 6288384 | bytes 6414336 | tf_op jit(solution)/shard_map/while/body/eval_jaxpr/reduce_sum | solution.py:55
  241.3 4.7 %bitcast_add_fusion.4 = f32[192,2,8,128]{3,0,2,1:T(8,128)} fusion(f32[192,2,8,128]{3,0,2,1:T(8,128)} %get-tuple-element.252, f32[2,512,192,8]{1,2,3,0:T(8,128)S(1)} %copy-done.1, f32[192,2,8]{0,2,1:T(8,128)S(1)} %select_maximum_fusion.2, pred[192,512]{1,0:T(8,128)(4,1)S(1)} %compare_and_fusion.2, f32[192,2,8]{0,2,1:T(8,128)S(1)} %get-tuple-element.233, ...), kind=kOutput, calls=%fused_computation.14.clone.1 | convolution fusion | flops 410124288 | bytes 9822209 | tf_op jit(solution)/shard_map/while/body/eval_jaxpr/qkgs,skd->qkgd/dot_general | solution.py:57
  252.6 3.7 fusion.60
  256.4 4.3 %fusion.61 = f32[192,2,8]{0,2,1:T(8,128)S(1)} fusion(f32[2,512,192,8]{1,2,3,0:T(8,128)} %get-tuple-element.231, f32[192,2,8]{0,2,1:T(8,128)S(1)} %select_maximum_fusion.2, pred[192,512]{1,0:T(8,128)(4,1)S(1)} %compare_and_fusion.2), kind=kLoop, calls=%fused_computation.8.clone.1 | loop fusion | flops 6288384 | bytes 6414336 | tf_op jit(solution)/shard_map/while/body/eval_jaxpr/reduce_sum | solution.py:55
  261.0 4.5 %bitcast_add_fusion.4 = f32[192,2,8,128]{3,0,2,1:T(8,128)} fusion(f32[192,2,8,128]{3,0,2,1:T(8,128)} %get-tuple-element.252, f32[2,512,192,8]{1,2,3,0:T(8,128)S(1)} %copy-done.1, f32[192,2,8]{0,2,1:T(8,128)S(1)} %select_maximum_fusion.2, pred[192,512]{1,0:T(8,128)(4,1)S(1)} %compare_and_fusion.2, f32[192,2,8]{0,2,1:T(8,128)S(1)} %get-tuple-element.233, ...), kind=kOutput, calls=%fused_computation.14.clone.1 | convolution fusion | flops 410124288 | bytes 9822209 | tf_op jit(solution)/shard_map/while/body/eval_jaxpr/qkgs,skd->qkgd/dot_general | solution.py:57
  272.2 3.7 fusion.60
  275.9 4.3 %fusion.61 = f32[192,2,8]{0,2,1:T(8,128)S(1)} fusion(f32[2,512,192,8]{1,2,3,0:T(8,128)} %get-tuple-element.231, f32[192,2,8]{0,2,1:T(8,128)S(1)} %select_maximum_fusion.2, pred[192,512]{1,0:T(8,128)(4,1)S(1)} %compare_and_fusion.2), kind=kLoop, calls=%fused_computation.8.clone.1 | loop fusion | flops 6288384 | bytes 6414336 | tf_op jit(solution)/shard_map/while/body/eval_jaxpr/reduce_sum | solution.py:55
  280.7 4.5 %bitcast_add_fusion.4 = f32[192,2,8,128]{3,0,2,1:T(8,128)} fusion(f32[192,2,8,128]{3,0,2,1:T(8,128)} %get-tuple-element.252, f32[2,512,192,8]{1,2,3,0:T(8,128)S(1)} %copy-done.1, f32[192,2,8]{0,2,1:T(8,128)S(1)} %select_maximum_fusion.2, pred[192,512]{1,0:T(8,128)(4,1)S(1)} %compare_and_fusion.2, f32[192,2,8]{0,2,1:T(8,128)S(1)} %get-tuple-element.233, ...), kind=kOutput, calls=%fused_computation.14.clone.1 | convolution fusion | flops 410124288 | bytes 9822209 | tf_op jit(solution)/shard_map/while/body/eval_jaxpr/qkgs,skd->qkgd/dot_general | solution.py:57
  291.8 3.7 fusion.60
  295.6 4.3 %fusion.61 = f32[192,2,8]{0,2,1:T(8,128)S(1)} fusion(f32[2,512,192,8]{1,2,3,0:T(8,128)} %get-tuple-element.231, f32[192,2,8]{0,2,1:T(8,128)S(1)} %select_maximum_fusion.2, pred[192,512]{1,0:T(8,128)(4,1)S(1)} %compare_and_fusion.2), kind=kLoop, calls=%fused_computation.8.clone.1 | loop fusion | flops 6288384 | bytes 6414336 | tf_op jit(solution)/shard_map/while/body/eval_jaxpr/reduce_sum | solution.py:55
  300.2 4.5 %bitcast_add_fusion.4 = f32[192,2,8,128]{3,0,2,1:T(8,128)} fusion(f32[192,2,8,128]{3,0,2,1:T(8,128)} %get-tuple-element.252, f32[2,512,192,8]{1,2,3,0:T(8,128)S(1)} %copy-done.1, f32[192,2,8]{0,2,1:T(8,128)S(1)} %select_maximum_fusion.2, pred[192,512]{1,0:T(8,128)(4,1)S(1)} %compare_and_fusion.2, f32[192,2,8]{0,2,1:T(8,128)S(1)} %get-tuple-element.233, ...), kind=kOutput, calls=%fused_computation.14.clone.1 | convolution fusion | flops 410124288 | bytes 9822209 | tf_op jit(solution)/shard_map/while/body/eval_jaxpr/qkgs,skd->qkgd/dot_general | solution.py:57
  307.2 11.3 %all-gather.8.cloned.1.call-done = bf16[2048,1024]{1,0:T(8,128)(2,1)} async-done(((bf16[128,1024]{1,0:T(8,128)(2,1)}), bf16[2048,1024]{1,0:T(8,128)(2,1)}) %all-gather.8.cloned.1.call-update) | async-done | bytes 4194320 | tf_op jit(solution)/shard_map/all_gather | solution.py:82
  322.3 25.8 %all_to_all.10 = bf16[16,24,1024]{2,1,0:T(8,128)(2,1)S(1)} all-to-all(bf16[16,24,1024]{2,1,0:T(8,128)(2,1)S(1)} %bitcast.127), channel_id=1, replica_groups=mesh['ctx'=16,'exp'=16,'dp'=2] {'exp'}, dimensions={0} | all-to-all | bytes 1572864 | tf_op jit(solution)/shard_map/all_to_all | solution.py:112
  355.9 20.9 %all-to-all-done.1 = bf16[16,24,1024]{2,1,0:T(8,128)(2,1)S(1)} async-done(((bf16[16,24,1024]{2,1,0:T(8,128)(2,1)}), bf16[16,24,1024]{2,1,0:T(8,128)(2,1)S(1)}, u32[]{:S(2)}, u32[]{:S(2)}) %all-to-all-start.1) | async-done | bytes 786464 | tf_op jit(solution)/shard_map/all_to_all | solution.py:121
  376.9 5.8 %gather_fusion = bf16[1536,1024]{1,0:T(8,128)(2,1)} fusion(bf16[385,1024]{1,0:T(8,128)(2,1)S(1)} %concatenate.3, s32[2048]{0:T(1024)S(1)} %pad_clamp_fusion), kind=kCustom, calls=%fused_computation | custom fusion | bytes 6297600 | tf_op jit(solution)/shard_map/gather | solution.py:132
  (133 shorter events, 70.8 us)
Async XLA Ops:
  6.5 342.2 %copy-start = (bf16[1,384,1024]{2,1,0:T(8,128)(2,1)S(1)}, bf16[1,384,1024]{2,1,0:T(8,128)(2,1)}, u32[]{:S(2)}) copy-start(bf16[1,384,1024]{2,1,0:T(8,128)(2,1)} %param.25) | copy-start | bytes 2359300
  6.5 94.1 %all-gather.6.cloned.1.call-start = ((), (), s32[]{:S(2)}) async-start(), calls=%async_computation.3 | async-start | bytes 1671168 | tf_op jit(solution)/shard_map/all_gather | solution.py:70
  7.3 177.6 %all-gather.4.cloned.1.call-start = ((), (), s32[]{:S(2)}) async-start(), calls=%async_computation.2 | async-start | bytes 1671168 | tf_op jit(solution)/shard_map/all_gather | solution.py:69
  8.0 310.5 %all-gather.8.cloned.1.call-start = ((), (), s32[]{:S(2)}) async-start(), calls=%async_computation.4 | async-start | bytes 4456448 | tf_op jit(solution)/shard_map/all_gather | solution.py:82
  9.6 9.6 %copy-start.2 = (s32[1,192,8]{2,1,0:T(8,128)}, s32[1,192,8]{2,1,0:T(8,128)S(1)}, u32[]{:S(2)}) copy-start(s32[1,192,8]{2,1,0:T(8,128)S(1)} %copy.27) | copy-start | bytes 18436
  15.7 0.6 copy-start.6
  198.7 4.9 %copy-start.1 = (f32[2,512,192,8]{1,2,3,0:T(8,128)S(1)}, f32[2,512,192,8]{1,2,3,0:T(8,128)}, u32[]{:S(2)}) copy-start(f32[2,512,192,8]{1,2,3,0:T(8,128)} %get-tuple-element.231) | copy-start | bytes 18874372 | tf_op jit(solution)/shard_map/while
  217.1 4.7 %copy-start.1 = (f32[2,512,192,8]{1,2,3,0:T(8,128)S(1)}, f32[2,512,192,8]{1,2,3,0:T(8,128)}, u32[]{:S(2)}) copy-start(f32[2,512,192,8]{1,2,3,0:T(8,128)} %get-tuple-element.231) | copy-start | bytes 18874372 | tf_op jit(solution)/shard_map/while
  236.7 4.6 %copy-start.1 = (f32[2,512,192,8]{1,2,3,0:T(8,128)S(1)}, f32[2,512,192,8]{1,2,3,0:T(8,128)}, u32[]{:S(2)}) copy-start(f32[2,512,192,8]{1,2,3,0:T(8,128)} %get-tuple-element.231) | copy-start | bytes 18874372 | tf_op jit(solution)/shard_map/while
  256.4 4.6 %copy-start.1 = (f32[2,512,192,8]{1,2,3,0:T(8,128)S(1)}, f32[2,512,192,8]{1,2,3,0:T(8,128)}, u32[]{:S(2)}) copy-start(f32[2,512,192,8]{1,2,3,0:T(8,128)} %get-tuple-element.231) | copy-start | bytes 18874372 | tf_op jit(solution)/shard_map/while
  275.9 4.7 %copy-start.1 = (f32[2,512,192,8]{1,2,3,0:T(8,128)S(1)}, f32[2,512,192,8]{1,2,3,0:T(8,128)}, u32[]{:S(2)}) copy-start(f32[2,512,192,8]{1,2,3,0:T(8,128)} %get-tuple-element.231) | copy-start | bytes 18874372 | tf_op jit(solution)/shard_map/while
  295.6 4.6 %copy-start.1 = (f32[2,512,192,8]{1,2,3,0:T(8,128)S(1)}, f32[2,512,192,8]{1,2,3,0:T(8,128)}, u32[]{:S(2)}) copy-start(f32[2,512,192,8]{1,2,3,0:T(8,128)} %get-tuple-element.231) | copy-start | bytes 18874372 | tf_op jit(solution)/shard_map/while
  304.8 13.8 %copy-start.10 = (bf16[1,192,1024]{2,1,0:T(8,128)(2,1)S(1)}, bf16[1,192,1024]{2,1,0:T(8,128)(2,1)}, u32[]{:S(2)}) copy-start(bf16[1,192,1024]{2,1,0:T(8,128)(2,1)} %param.18) | copy-start | bytes 1179652
  318.5 3.3 copy-start.5
  318.5 3.3 copy-start.9
  321.8 26.3 %copy-start.4 = (bf16[1,1024,384]{2,1,0:T(8,128)(2,1)S(1)}, bf16[1,1024,384]{2,1,0:T(8,128)(2,1)}, u32[]{:S(2)}) copy-start(bf16[1,1024,384]{2,1,0:T(8,128)(2,1)} %param.23) | copy-start | bytes 2359300
  348.7 6.7 %copy-start.7 = (s32[1536]{0:T(1024)S(1)}, s32[1536]{0:T(1024)}, u32[]{:S(2)}) copy-start(s32[1536]{0:T(1024)} %copy-done.6) | copy-start | bytes 18436
  348.7 6.9 %copy-start.3 = (s32[1,192,8]{2,1,0:T(8,128)S(1)}, s32[1,192,8]{2,1,0:T(8,128)}, u32[]{:S(2)}) copy-start(s32[1,192,8]{2,1,0:T(8,128)} %copy-done.2) | copy-start | bytes 18436
  348.7 7.0 %copy-start.8 = (f32[1,192,8]{1,2,0:T(8,128)S(1)}, f32[1,192,8]{1,2,0:T(8,128)}, u32[]{:S(2)}) copy-start(f32[1,192,8]{1,2,0:T(8,128)} %param.22) | copy-start | bytes 18436
  351.8 25.0 %all-to-all-start.1 = ((bf16[16,24,1024]{2,1,0:T(8,128)(2,1)}), bf16[16,24,1024]{2,1,0:T(8,128)(2,1)S(1)}, u32[]{:S(2)}, u32[]{:S(2)}) async-start(bf16[16,24,1024]{2,1,0:T(8,128)(2,1)} %bitcast.13), calls=%async_computation.1 | async-start | bytes 1572864 | tf_op jit(solution)/shard_map/all_to_all | solution.py:121
Sparse Core Ops, SparseCore 0:
  10.4 90.1 all-gather.5
  103.7 81.1 all-gather.3
  187.9 130.5 all-gather.7
where the time goes:
time: 395 us; the launch traced here: 393 us
  waiting for transfers between devices  196 us (50%)
  matrix products  58.6 us (15%)
  other arithmetic  44.6 us (11%)
  local copies, waits for them, and re-layouts  39.7 us (10%)
  blocking collectives  25.8 us (7%)
  between operations  13.4 us (3%)
  loops' own time  11.2 us (3%)
    all_gather x1, waiting for transfers between devices, per_device(): key_piece = lax.all_gather(keys, 'ctx', axis=1, tiled=True)  81.9 us
    all_gather x1, waiting for transfers between devices, per_device(): value_piece = lax.all_gather(values, 'ctx', axis=1, tiled=True)  79.8 us
    reduce_sum x6, other arithmetic, attend_block(): new_sum = run_sum * correction + jnp.sum(expo, axis=-1)  26 us
    dot_general x6, matrix products, attend_block(): jnp.einsum('qkgs,skd->qkgd', probs, value_blk, preferred_element_type=jnp...  25.9 us
    all_to_all x1, blocking collectives, per_device(): lax.all_to_all(outgoing, 'exp', split_axis=0, concat_axis=0, tiled=True)  25.8 us
    dot_general x6, matrix products, attend_block(): jnp.einsum('qkgd,skd->qkgs', query_heads, key_blk, preferred_element_type...  22.4 us
    all_to_all x1, waiting for transfers between devices, per_device(): lax.all_to_all(expert_out.reshape(owners, item_count, model_width), 'exp'...  20.9 us
    dynamic_slice x12, local copies, waits for them, and re-layouts, per_device(): lax.scan(attend_block, running, (key_blocks, value_blocks, blk_starts))  15.4 us
  transfers between devices with their start and end apart: 4, of which 4 were waited for; matrix products, arithmetic and copies ran while one was open for 31% of the time, Pallas kernels for 0%

commit v1 on v0

--- a/solution.py
+++ b/solution.py
@@ -67,7 +67,9 @@
     )
     running = initial
     key_piece = lax.all_gather(keys, "ctx", axis=1, tiled=True)
-    value_piece = lax.all_gather(values, "ctx", axis=1, tiled=True)
+    value_piece = jnp.concatenate(
+        lax.all_to_all(jnp.stack([values] * lax.axis_size("ctx")), "ctx", 0, 0), axis=1
+    )
     row_count = key_piece.shape[1]
     blk_rows = math.gcd(row_count, 512)
     blk_count = row_count // blk_rows

time: 395 us -> 365 us (0.924)
  waiting for transfers between devices: 196 us -> 159 us
  starting transfers between devices: 3.69 us -> 22.1 us
  other arithmetic: 44.6 us -> 39.3 us
    all_gather x1 -> x0, waiting for transfers between devices: 79.8 us -> none  [per_device(): value_piece = lax.all_gather(values, 'ctx', axis=1, tiled=True)]
    all_gather x1, waiting for transfers between devices: 81.9 us -> 118 us  [per_device(): key_piece = lax.all_gather(keys, 'ctx', axis=1, tiled=True)]
    all_to_all x0 -> x1, starting transfers between devices: none -> 18.4 us  [per_device(): lax.all_to_all(jnp.stack([values] * lax.axis_size('ctx')), 'ctx', 0, 0)]
    all_gather x1, waiting for transfers between devices: 11.3 us -> 18.7 us  [per_device(): lax.all_gather(out_weight, 'ctx', axis=0, tiled=True)]
    and x6, other arithmetic: 4.96 us -> 0.89 us  [attend_block(): (key_pos[None, :] <= query_pos[:, None]) & (key_seg[None, :] == query_seg...]
  transfers between devices with their start and end apart: 4 -> 4, of which waited for: 4 -> 3; matrix products, arithmetic and copies ran while one was open for 31% -> 31% of each run, Pallas kernels for 0% -> 0%
where the time goes in v1:
time: 365 us; the launch traced here: 364 us
  waiting for transfers between devices  159 us (44%)
  matrix products  58.4 us (16%)
  other arithmetic  39.3 us (11%)
  local copies, waits for them, and re-layouts  35.9 us (10%)
  blocking collectives  25.7 us (7%)
  starting transfers between devices  22.1 us (6%)
  between operations  13.7 us (4%)
  loops' own time  10.3 us (3%)
    all_gather x1, waiting for transfers between devices, per_device(): key_piece = lax.all_gather(keys, 'ctx', axis=1, tiled=True)  118 us
    reduce_sum x6, other arithmetic, attend_block(): new_sum = run_sum * correction + jnp.sum(expo, axis=-1)  26.3 us
    all_to_all x1, blocking collectives, per_device(): lax.all_to_all(outgoing, 'exp', split_axis=0, concat_axis=0, tiled=True)  25.7 us
    dot_general x6, matrix products, attend_block(): jnp.einsum('qkgs,skd->qkgd', probs, value_blk, preferred_element_type=jnp...  25.6 us
    dot_general x6, matrix products, attend_block(): jnp.einsum('qkgd,skd->qkgs', query_heads, key_blk, preferred_element_type...  22.5 us
    all_to_all x1, waiting for transfers between devices, per_device(): lax.all_to_all(expert_out.reshape(owners, item_count, model_width), 'exp'...  20.9 us
    all_gather x1, waiting for transfers between devices, per_device(): lax.all_gather(out_weight, 'ctx', axis=0, tiled=True)  18.7 us
    all_to_all x1, starting transfers between devices, per_device(): lax.all_to_all(jnp.stack([values] * lax.axis_size('ctx')), 'ctx', 0, 0)  18.4 us
  transfers between devices with their start and end apart: 4, of which 3 were waited for; matrix products, arithmetic and copies ran while one was open for 31% of the time, Pallas kernels for 0%

profile of v1, /device:TPU:1, one launch (start us, length us, event | category | flops | bytes accessed | tf_op | source)
XLA Modules:
  0.0 364.0 jit_solution(7091263549598697016)
XLA Ops:
  8.9 18.4 %all-to-all-start = ((bf16[16,1,192,256]{3,2,1,0:T(8,128)(2,1)}), bf16[16,1,192,256]{3,2,1,0:T(8,128)(2,1)S(1)}, u32[]{:S(2)}, u32[]{:S(2)}) async-start(bf16[16,1,192,256]{3,2,1,0:T(8,128)(2,1)} %stack.2), calls=%async_computation | async-start | bytes 3145728 | tf_op jit(solution)/shard_map/all_to_all | solution.py:71
  29.2 4.5 %reduce-window.6 = s32[16,12,128]{2,1,0:T(8,128)S(1)} reduce-window(s32[16,12,128]{2,1,0:T(8,128)S(1)} %fusion.41, s32[]{:T(128)} %constant.11.clone.1), window={size=1x1x128 pad=0_0x0_0x127_0}, to_apply=%region_4.5 | reduce-window | flops 3121152 | bytes 196612 | tf_op jit(solution)/shard_map/reduce-window
  37.7 117.6 %all-gather.3.cloned.1.call-done = bf16[1,3072,256]{2,1,0:T(8,128)(2,1)} async-done(((bf16[1,192,256]{2,1,0:T(8,128)(2,1)}), bf16[1,3072,256]{2,1,0:T(8,128)(2,1)}) %all-gather.3.cloned.1.call-update) | async-done | bytes 1572880 | tf_op jit(solution)/shard_map/all_gather | solution.py:69
  160.7 107.5 %while.15 = (s32[]{:T(128)}, f32[192,2,8]{0,2,1:T(8,128)S(1)}, f32[192,2,8]{0,2,1:T(8,128)S(1)}, f32[192,2,8,128]{3,0,2,1:T(8,128)}, s32[6]{0:T(128)S(1)}, /*ind...) while((s32[]{:T(128)}, f32[192,2,8]{0,2,1:T(8,128)S(1)}, ...), condition=%wide.region_3.4_spmd.clone, body=%wide.region_0.3_spmd.clone.sunk | while | flops 824098496 | bytes 50147816 | solution.py:79
  165.9 3.8 %fusion.60 = (f32[192,2,8]{0,2,1:T(8,128)S(1)}, f32[2,512,192,8]{1,2,3,0:T(8,128)}) fusion(pred[192,512]{1,0:T(8,128)(4,1)S(1)} %compare_and_fusion.2, bf16[192,2,8,128]{3,0,2,1:T(8,128)(2,1)S(1)} %get-tuple-element.282, bf16[1,512,2,128]{3,2,1,0:T(2,128)(2,1)S(1)} %get-tuple-element.240), kind=kOutput, calls=%fused_computation.4.clone.1 | convolution fusion | flops 407368704 | bytes 7450624 | tf_op jit(solution)/shard_map/while/body/eval_jaxpr/qkgd,skd->qkgs/dot_general | solution.py:45
  169.6 4.4 %fusion.61 = f32[192,2,8]{0,2,1:T(8,128)S(1)} fusion(f32[2,512,192,8]{1,2,3,0:T(8,128)} %get-tuple-element.242, f32[192,2,8]{0,2,1:T(8,128)S(1)} %select_maximum_fusion.2, pred[192,512]{1,0:T(8,128)(4,1)S(1)} %compare_and_fusion.2), kind=kLoop, calls=%fused_computation.8.clone.1 | loop fusion | flops 6288384 | bytes 6414336 | tf_op jit(solution)/shard_map/while/body/eval_jaxpr/reduce_sum | solution.py:55
  182.8 3.7 %fusion.60 = (f32[192,2,8]{0,2,1:T(8,128)S(1)}, f32[2,512,192,8]{1,2,3,0:T(8,128)}) fusion(pred[192,512]{1,0:T(8,128)(4,1)S(1)} %compare_and_fusion.2, bf16[192,2,8,128]{3,0,2,1:T(8,128)(2,1)S(1)} %get-tuple-element.282, bf16[1,512,2,128]{3,2,1,0:T(2,128)(2,1)S(1)} %get-tuple-element.240), kind=kOutput, calls=%fused_computation.4.clone.1 | convolution fusion | flops 407368704 | bytes 7450624 | tf_op jit(solution)/shard_map/while/body/eval_jaxpr/qkgd,skd->qkgs/dot_general | solution.py:45
  186.5 4.4 %fusion.61 = f32[192,2,8]{0,2,1:T(8,128)S(1)} fusion(f32[2,512,192,8]{1,2,3,0:T(8,128)} %get-tuple-element.242, f32[192,2,8]{0,2,1:T(8,128)S(1)} %select_maximum_fusion.2, pred[192,512]{1,0:T(8,128)(4,1)S(1)} %compare_and_fusion.2), kind=kLoop, calls=%fused_computation.8.clone.1 | loop fusion | flops 6288384 | bytes 6414336 | tf_op jit(solution)/shard_map/while/body/eval_jaxpr/reduce_sum | solution.py:55
  191.2 4.5 %bitcast_add_fusion.4 = f32[192,2,8,128]{3,0,2,1:T(8,128)} fusion(f32[192,2,8,128]{3,0,2,1:T(8,128)} %get-tuple-element.263, f32[2,512,192,8]{1,2,3,0:T(8,128)S(1)} %copy-done.1, f32[192,2,8]{0,2,1:T(8,128)S(1)} %select_maximum_fusion.2, pred[192,512]{1,0:T(8,128)(4,1)S(1)} %compare_and_fusion.2, f32[192,2,8]{0,2,1:T(8,128)S(1)} %get-tuple-element.244, ...), kind=kOutput, calls=%fused_computation.14.clone.1 | convolution fusion | flops 410124288 | bytes 9822209 | tf_op jit(solution)/shard_map/while/body/eval_jaxpr/qkgs,skd->qkgd/dot_general | solution.py:57
  204.6 4.4 %fusion.61 = f32[192,2,8]{0,2,1:T(8,128)S(1)} fusion(f32[2,512,192,8]{1,2,3,0:T(8,128)} %get-tuple-element.242, f32[192,2,8]{0,2,1:T(8,128)S(1)} %select_maximum_fusion.2, pred[192,512]{1,0:T(8,128)(4,1)S(1)} %compare_and_fusion.2), kind=kLoop, calls=%fused_computation.8.clone.1 | loop fusion | flops 6288384 | bytes 6414336 | tf_op jit(solution)/shard_map/while/body/eval_jaxpr/reduce_sum | solution.py:55
  209.3 4.5 %bitcast_add_fusion.4 = f32[192,2,8,128]{3,0,2,1:T(8,128)} fusion(f32[192,2,8,128]{3,0,2,1:T(8,128)} %get-tuple-element.263, f32[2,512,192,8]{1,2,3,0:T(8,128)S(1)} %copy-done.1, f32[192,2,8]{0,2,1:T(8,128)S(1)} %select_maximum_fusion.2, pred[192,512]{1,0:T(8,128)(4,1)S(1)} %compare_and_fusion.2, f32[192,2,8]{0,2,1:T(8,128)S(1)} %get-tuple-element.244, ...), kind=kOutput, calls=%fused_computation.14.clone.1 | convolution fusion | flops 410124288 | bytes 9822209 | tf_op jit(solution)/shard_map/while/body/eval_jaxpr/qkgs,skd->qkgd/dot_general | solution.py:57
  219.0 3.8 %fusion.60 = (f32[192,2,8]{0,2,1:T(8,128)S(1)}, f32[2,512,192,8]{1,2,3,0:T(8,128)}) fusion(pred[192,512]{1,0:T(8,128)(4,1)S(1)} %compare_and_fusion.2, bf16[192,2,8,128]{3,0,2,1:T(8,128)(2,1)S(1)} %get-tuple-element.282, bf16[1,512,2,128]{3,2,1,0:T(2,128)(2,1)S(1)} %get-tuple-element.240), kind=kOutput, calls=%fused_computation.4.clone.1 | convolution fusion | flops 407368704 | bytes 7450624 | tf_op jit(solution)/shard_map/while/body/eval_jaxpr/qkgd,skd->qkgs/dot_general | solution.py:45
  222.7 4.4 %fusion.61 = f32[192,2,8]{0,2,1:T(8,128)S(1)} fusion(f32[2,512,192,8]{1,2,3,0:T(8,128)} %get-tuple-element.242, f32[192,2,8]{0,2,1:T(8,128)S(1)} %select_maximum_fusion.2, pred[192,512]{1,0:T(8,128)(4,1)S(1)} %compare_and_fusion.2), kind=kLoop, calls=%fused_computation.8.clone.1 | loop fusion | flops 6288384 | bytes 6414336 | tf_op jit(solution)/shard_map/while/body/eval_jaxpr/reduce_sum | solution.py:55
  227.4 4.5 %bitcast_add_fusion.4 = f32[192,2,8,128]{3,0,2,1:T(8,128)} fusion(f32[192,2,8,128]{3,0,2,1:T(8,128)} %get-tuple-element.263, f32[2,512,192,8]{1,2,3,0:T(8,128)S(1)} %copy-done.1, f32[192,2,8]{0,2,1:T(8,128)S(1)} %select_maximum_fusion.2, pred[192,512]{1,0:T(8,128)(4,1)S(1)} %compare_and_fusion.2, f32[192,2,8]{0,2,1:T(8,128)S(1)} %get-tuple-element.244, ...), kind=kOutput, calls=%fused_computation.14.clone.1 | convolution fusion | flops 410124288 | bytes 9822209 | tf_op jit(solution)/shard_map/while/body/eval_jaxpr/qkgs,skd->qkgd/dot_general | solution.py:57
  237.1 3.8 %fusion.60 = (f32[192,2,8]{0,2,1:T(8,128)S(1)}, f32[2,512,192,8]{1,2,3,0:T(8,128)}) fusion(pred[192,512]{1,0:T(8,128)(4,1)S(1)} %compare_and_fusion.2, bf16[192,2,8,128]{3,0,2,1:T(8,128)(2,1)S(1)} %get-tuple-element.282, bf16[1,512,2,128]{3,2,1,0:T(2,128)(2,1)S(1)} %get-tuple-element.240), kind=kOutput, calls=%fused_computation.4.clone.1 | convolution fusion | flops 407368704 | bytes 7450624 | tf_op jit(solution)/shard_map/while/body/eval_jaxpr/qkgd,skd->qkgs/dot_general | solution.py:45
  240.8 4.4 %fusion.61 = f32[192,2,8]{0,2,1:T(8,128)S(1)} fusion(f32[2,512,192,8]{1,2,3,0:T(8,128)} %get-tuple-element.242, f32[192,2,8]{0,2,1:T(8,128)S(1)} %select_maximum_fusion.2, pred[192,512]{1,0:T(8,128)(4,1)S(1)} %compare_and_fusion.2), kind=kLoop, calls=%fused_computation.8.clone.1 | loop fusion | flops 6288384 | bytes 6414336 | tf_op jit(solution)/shard_map/while/body/eval_jaxpr/reduce_sum | solution.py:55
  245.4 4.5 %bitcast_add_fusion.4 = f32[192,2,8,128]{3,0,2,1:T(8,128)} fusion(f32[192,2,8,128]{3,0,2,1:T(8,128)} %get-tuple-element.263, f32[2,512,192,8]{1,2,3,0:T(8,128)S(1)} %copy-done.1, f32[192,2,8]{0,2,1:T(8,128)S(1)} %select_maximum_fusion.2, pred[192,512]{1,0:T(8,128)(4,1)S(1)} %compare_and_fusion.2, f32[192,2,8]{0,2,1:T(8,128)S(1)} %get-tuple-element.244, ...), kind=kOutput, calls=%fused_computation.14.clone.1 | convolution fusion | flops 410124288 | bytes 9822209 | tf_op jit(solution)/shard_map/while/body/eval_jaxpr/qkgs,skd->qkgd/dot_general | solution.py:57
  255.1 3.7 %fusion.60 = (f32[192,2,8]{0,2,1:T(8,128)S(1)}, f32[2,512,192,8]{1,2,3,0:T(8,128)}) fusion(pred[192,512]{1,0:T(8,128)(4,1)S(1)} %compare_and_fusion.2, bf16[192,2,8,128]{3,0,2,1:T(8,128)(2,1)S(1)} %get-tuple-element.282, bf16[1,512,2,128]{3,2,1,0:T(2,128)(2,1)S(1)} %get-tuple-element.240), kind=kOutput, calls=%fused_computation.4.clone.1 | convolution fusion | flops 407368704 | bytes 7450624 | tf_op jit(solution)/shard_map/while/body/eval_jaxpr/qkgd,skd->qkgs/dot_general | solution.py:45
  258.9 4.4 %fusion.61 = f32[192,2,8]{0,2,1:T(8,128)S(1)} fusion(f32[2,512,192,8]{1,2,3,0:T(8,128)} %get-tuple-element.242, f32[192,2,8]{0,2,1:T(8,128)S(1)} %select_maximum_fusion.2, pred[192,512]{1,0:T(8,128)(4,1)S(1)} %compare_and_fusion.2), kind=kLoop, calls=%fused_computation.8.clone.1 | loop fusion | flops 6288384 | bytes 6414336 | tf_op jit(solution)/shard_map/while/body/eval_jaxpr/reduce_sum | solution.py:55
  263.6 4.5 %bitcast_add_fusion.4 = f32[192,2,8,128]{3,0,2,1:T(8,128)} fusion(f32[192,2,8,128]{3,0,2,1:T(8,128)} %get-tuple-element.263, f32[2,512,192,8]{1,2,3,0:T(8,128)S(1)} %copy-done.1, f32[192,2,8]{0,2,1:T(8,128)S(1)} %select_maximum_fusion.2, pred[192,512]{1,0:T(8,128)(4,1)S(1)} %compare_and_fusion.2, f32[192,2,8]{0,2,1:T(8,128)S(1)} %get-tuple-element.244, ...), kind=kOutput, calls=%fused_computation.14.clone.1 | convolution fusion | flops 410124288 | bytes 9822209 | tf_op jit(solution)/shard_map/while/body/eval_jaxpr/qkgs,skd->qkgd/dot_general | solution.py:57
  270.7 18.7 %all-gather.5.cloned.1.call-done = bf16[2048,1024]{1,0:T(8,128)(2,1)} async-done(((bf16[128,1024]{1,0:T(8,128)(2,1)}), bf16[2048,1024]{1,0:T(8,128)(2,1)}) %all-gather.5.cloned.1.call-update) | async-done | bytes 4194320 | tf_op jit(solution)/shard_map/all_gather | solution.py:84
  293.1 25.7 %all_to_all.15 = bf16[16,24,1024]{2,1,0:T(8,128)(2,1)S(1)} all-to-all(bf16[16,24,1024]{2,1,0:T(8,128)(2,1)S(1)} %bitcast.130), channel_id=1, replica_groups=mesh['ctx'=16,'exp'=16,'dp'=2] {'exp'}, dimensions={0} | all-to-all | bytes 1572864 | tf_op jit(solution)/shard_map/all_to_all | solution.py:114
  326.5 20.9 %all-to-all-done.2 = bf16[16,24,1024]{2,1,0:T(8,128)(2,1)S(1)} async-done(((bf16[16,24,1024]{2,1,0:T(8,128)(2,1)}), bf16[16,24,1024]{2,1,0:T(8,128)(2,1)S(1)}, u32[]{:S(2)}, u32[]{:S(2)}) %all-to-all-start.2) | async-done | bytes 786464 | tf_op jit(solution)/shard_map/all_to_all | solution.py:123
  347.5 5.8 %gather_fusion = bf16[1536,1024]{1,0:T(8,128)(2,1)} fusion(bf16[385,1024]{1,0:T(8,128)(2,1)S(1)} %concatenate.3, s32[2048]{0:T(1024)S(1)} %pad_clamp_fusion), kind=kCustom, calls=%fused_computation | custom fusion | bytes 6297600 | tf_op jit(solution)/shard_map/gather | solution.py:134
  (129 shorter events, 60.7 us)
Async XLA Ops:
  6.5 312.9 %copy-start = (bf16[1,384,1024]{2,1,0:T(8,128)(2,1)S(1)}, bf16[1,384,1024]{2,1,0:T(8,128)(2,1)}, u32[]{:S(2)}) copy-start(bf16[1,384,1024]{2,1,0:T(8,128)(2,1)} %param.25) | copy-start | bytes 2359300
  6.5 22.2 %copy-start.5 = (s32[1,192,8]{1,2,0:T(8,128)S(1)}, s32[1,192,8]{1,2,0:T(8,128)}, u32[]{:S(2)}) copy-start(s32[1,192,8]{1,2,0:T(8,128)} %param.21) | copy-start | bytes 18436
  8.9 149.9 %all-to-all-start = ((bf16[16,1,192,256]{3,2,1,0:T(8,128)(2,1)}), bf16[16,1,192,256]{3,2,1,0:T(8,128)(2,1)S(1)}, u32[]{:S(2)}, u32[]{:S(2)}) async-start(bf16[16,1,192,256]{3,2,1,0:T(8,128)(2,1)} %stack.2), calls=%async_computation | async-start | bytes 3145728 | tf_op jit(solution)/shard_map/all_to_all | solution.py:71
  27.3 128.0 %all-gather.3.cloned.1.call-start = ((), (), s32[]{:S(2)}) async-start(), calls=%async_computation.3 | async-start | bytes 1671168 | tf_op jit(solution)/shard_map/all_gather | solution.py:69
  28.0 261.3 %all-gather.5.cloned.1.call-start = ((), (), s32[]{:S(2)}) async-start(), calls=%async_computation.4 | async-start | bytes 4456448 | tf_op jit(solution)/shard_map/all_gather | solution.py:84
  169.6 4.9 %copy-start.1 = (f32[2,512,192,8]{1,2,3,0:T(8,128)S(1)}, f32[2,512,192,8]{1,2,3,0:T(8,128)}, u32[]{:S(2)}) copy-start(f32[2,512,192,8]{1,2,3,0:T(8,128)} %get-tuple-element.242) | copy-start | bytes 18874372 | tf_op jit(solution)/shard_map/while
  186.5 4.7 %copy-start.1 = (f32[2,512,192,8]{1,2,3,0:T(8,128)S(1)}, f32[2,512,192,8]{1,2,3,0:T(8,128)}, u32[]{:S(2)}) copy-start(f32[2,512,192,8]{1,2,3,0:T(8,128)} %get-tuple-element.242) | copy-start | bytes 18874372 | tf_op jit(solution)/shard_map/while
  204.6 4.6 %copy-start.1 = (f32[2,512,192,8]{1,2,3,0:T(8,128)S(1)}, f32[2,512,192,8]{1,2,3,0:T(8,128)}, u32[]{:S(2)}) copy-start(f32[2,512,192,8]{1,2,3,0:T(8,128)} %get-tuple-element.242) | copy-start | bytes 18874372 | tf_op jit(solution)/shard_map/while
  222.7 4.7 %copy-start.1 = (f32[2,512,192,8]{1,2,3,0:T(8,128)S(1)}, f32[2,512,192,8]{1,2,3,0:T(8,128)}, u32[]{:S(2)}) copy-start(f32[2,512,192,8]{1,2,3,0:T(8,128)} %get-tuple-element.242) | copy-start | bytes 18874372 | tf_op jit(solution)/shard_map/while
  240.8 4.6 %copy-start.1 = (f32[2,512,192,8]{1,2,3,0:T(8,128)S(1)}, f32[2,512,192,8]{1,2,3,0:T(8,128)}, u32[]{:S(2)}) copy-start(f32[2,512,192,8]{1,2,3,0:T(8,128)} %get-tuple-element.242) | copy-start | bytes 18874372 | tf_op jit(solution)/shard_map/while
  258.9 4.8 %copy-start.1 = (f32[2,512,192,8]{1,2,3,0:T(8,128)S(1)}, f32[2,512,192,8]{1,2,3,0:T(8,128)}, u32[]{:S(2)}) copy-start(f32[2,512,192,8]{1,2,3,0:T(8,128)} %get-tuple-element.242) | copy-start | bytes 18874372 | tf_op jit(solution)/shard_map/while
  268.2 21.1 %copy-start.8 = (bf16[1,192,1024]{2,1,0:T(8,128)(2,1)S(1)}, bf16[1,192,1024]{2,1,0:T(8,128)(2,1)}, u32[]{:S(2)}) copy-start(bf16[1,192,1024]{2,1,0:T(8,128)(2,1)} %param.18) | copy-start | bytes 1179652
  289.3 3.3 copy-start.7
  292.6 26.2 %copy-start.2 = (f32[192,1024]{1,0:T(8,128)}, f32[192,1024]{1,0:T(8,128)S(1)}, u32[]{:S(2)}) copy-start(f32[192,1024]{1,0:T(8,128)S(1)} %get-tuple-element.166) | copy-start | bytes 2359300
  292.6 26.2 %copy-start.4 = (bf16[1,1024,384]{2,1,0:T(8,128)(2,1)S(1)}, bf16[1,1024,384]{2,1,0:T(8,128)(2,1)}, u32[]{:S(2)}) copy-start(bf16[1,1024,384]{2,1,0:T(8,128)(2,1)} %param.23) | copy-start | bytes 2359300
  319.4 6.9 %copy-start.6 = (f32[1,192,8]{1,2,0:T(8,128)S(1)}, f32[1,192,8]{1,2,0:T(8,128)}, u32[]{:S(2)}) copy-start(f32[1,192,8]{1,2,0:T(8,128)} %param.22) | copy-start | bytes 18436
  322.5 25.0 %all-to-all-start.2 = ((bf16[16,24,1024]{2,1,0:T(8,128)(2,1)}), bf16[16,24,1024]{2,1,0:T(8,128)(2,1)S(1)}, u32[]{:S(2)}, u32[]{:S(2)}) async-start(bf16[16,24,1024]{2,1,0:T(8,128)(2,1)} %bitcast.135), calls=%async_computation.2 | async-start | bytes 1572864 | tf_op jit(solution)/shard_map/all_to_all | solution.py:123
  353.3 2.9 copy-start.3
Sparse Core Ops, SparseCore 0:
  31.1 124.1 all-gather.2
  158.3 130.9 all-gather.4
